TPU v7x, 32 devices: a whole 2x2x4 slice. The times are simulated.
32 devices in a mesh: frame: 8 (over y, x, core), query: 4 (over z).
Axes of the slice: x: 2, y: 2, z: 4, core: 2. Of those that a mesh axis runs over, the one named last changes fastest.
Arguments:
- features: bfloat16 [8, 4096, 256], P('frame'), may hold values from -4.375 to 4.375
- kernel: float32 [3, 3], replicated, may hold values from 0.2 to 1
- cotangent: float32 [2, 8, 4096], P(None, 'frame', 'query'), may hold values from -6 to 6
- query_frame: int32 [4096], P('query'), may hold values from 0 to 7
- query_pixel: int32 [4096], P('query'), may hold values from 0 to 4095
Outputs:
- query_grad: float32 [4096, 256], P('query')
- feature_grad: float32 [8, 4096, 256], P('frame', 'query')
All inputs are finite; a program needn't handle non-finite values.
Results may differ from a plain program's by a relative error of at most 0.0029.
Values may be sent and summed in bfloat16 or wider, within the bound.
No kernel may reach another device: no remote copies, remote signals or barrier semaphores. Data moves between devices by JAX's collectives and lax.ppermute only.
A program may use at most 128 MiB of HBM per device.

v0:
```python
import jax
import jax.numpy as jnp
from jax import lax
from jax.sharding import PartitionSpec as P

W = 64


def shifted(values, offset, margin, length):
    padded = jnp.pad(values, ((0, 0), (margin, margin)))
    return lax.slice_in_dim(padded, margin + offset, margin + offset + length, axis=1)


def shards(features, kernel, cotangent, query_frame, query_pixel):
    t_dev, pixels, chan = features.shape
    height = pixels // W
    margin = W + 1
    frame_base = lax.axis_index("frame") * t_dev
    local_frame = query_frame - frame_base
    owned = (local_frame >= 0) & (local_frame < t_dev)
    flat_rows = jnp.clip(local_frame, 0, t_dev - 1) * pixels + query_pixel
    flat_maps = features.reshape(t_dev * pixels, chan)
    picked = jnp.where(owned[:, None], flat_maps[flat_rows], 0).astype(jnp.float32)
    qfeat = lax.psum(picked.astype(jnp.bfloat16), "frame")
    where_pix = lax.iota(jnp.int32, pixels)
    column = where_pix % W
    row_pos = (where_pix // W).astype(jnp.float32) - (height - 1) / 2.0
    col_pos = column.astype(jnp.float32) - (W - 1) / 2.0
    col_masks = {
        -1: (column >= 1)[None, :],
        0: (column >= 0)[None, :],
        1: (column <= W - 2)[None, :],
    }
    frame_map = features[0]
    cost = lax.dot_general(
        qfeat, frame_map, (((1,), (1,)), ((), ())), preferred_element_type=jnp.float32
    )
    logits = jnp.zeros_like(cost)
    for a in (-1, 0, 1):
        for b in (-1, 0, 1):
            moved = shifted(cost, a * W + b, margin, pixels)
            logits = logits + kernel[a + 1, b + 1] * jnp.where(col_masks[b], moved, 0.0)
    top = jnp.max(logits, axis=1, keepdims=True)
    expo = jnp.exp(logits - top)
    prob = expo / jnp.sum(expo, axis=1, keepdims=True)
    pull = cotangent[0, 0][:, None] * row_pos[None, :] + cotangent[1, 0][:, None] * col_pos[None, :]
    mean_pull = jnp.sum(prob * pull, axis=1, keepdims=True)
    dlogit = prob * (pull - mean_pull)
    dcost = jnp.zeros_like(dlogit)
    for a in (-1, 0, 1):
        for b in (-1, 0, 1):
            masked = jnp.where(col_masks[b], dlogit, 0.0)
            dcost = dcost + kernel[a + 1, b + 1] * shifted(masked, -(a * W + b), margin, pixels)
    dcost = dcost.astype(jnp.bfloat16)
    query_part = jnp.dot(dcost, frame_map, preferred_element_type=jnp.float32)
    frame_terms = [
        lax.dot_general(dcost, qfeat, (((0,), (0,)), ((), ())), preferred_element_type=jnp.float32)
    ]
    feature_term = jnp.stack(frame_terms)
    query_grad = lax.psum(query_part, "frame")
    placed = jnp.where(owned[:, None], query_grad, 0.0)
    feature_term = (
        feature_term.reshape(t_dev * pixels, chan)
        .at[flat_rows]
        .add(placed)
        .reshape(t_dev, pixels, chan)
    )
    feature_grad = lax.psum_scatter(feature_term, "query", scatter_dimension=1, tiled=True)
    return (query_grad, feature_grad)


def solution(mesh):
    placed = (P("frame", None, None), P(), P(None, "frame", "query"), P("query"), P("query"))
    return jax.shard_map(
        shards,
        mesh=mesh,
        in_specs=placed,
        out_specs=(P("query", None), P("frame", "query", None)),
        check_vma=False,
    )
```

profile of v0, /device:TPU:0, one launch (start us, length us, event | category | flops | bytes accessed | tf_op | source)
XLA Modules:
  0.0 449.0 jit_solution(2033591671652492786)
XLA Ops:
  7.2 0.0 copy-start
  7.2 0.0 all-reduce.7.cloned.1.call-start
  7.2 0.8 compare_and_fusion
  8.1 0.7 broadcast_clamp_fusion
  8.8 0.0 copy-done
  8.8 3.9 gather_fusion
  12.7 1.0 broadcast_select_fusion.3
  13.7 0.0 all-reduce.7.cloned.1.call-update
  13.8 0.0 all-reduce.9.cloned.1.call-start
  13.8 1.7 fusion.43
  15.5 0.7 fusion.42
  16.3 55.2 %all-reduce.7.cloned.1.call-done = bf16[1024,256]{1,0:T(8,128)(2,1)} async-done(((bf16[1024,256]{1,0:T(8,128)(2,1)}), bf16[1024,256]{1,0:T(8,128)(2,1)}) %all-reduce.7.cloned.1.call-update) | async-done | bytes 524304 | tf_op jit(solution)/shard_map/psum | solution.py:24
  71.4 9.1 %fusion.39 = f32[1024,4096]{1,0:T(8,128)} fusion(bf16[1024,256]{1,0:T(8,128)(2,1)} %all-reduce.7.cloned.1.call-done, bf16[1,4096,256]{2,1,0:T(8,128)(2,1)S(1)} %copy-done), kind=kOutput, calls=%fused_computation.66 | convolution fusion | flops 2147483648 | bytes 19398656 | tf_op jit(solution)/shard_map/dot_general | solution.py:35
  80.6 85.7 %fusion.41 = (f32[1024]{0:T(1024)S(1)}, f32[1024,4096]{1,0:T(8,128)}) fusion(f32[]{:T(128)} %bitcast.9, f32[]{:T(128)} %bitcast.8, f32[]{:T(128)} %bitcast.7, f32[]{:T(128)} %bitcast.6, f32[1024,4096]{1,0:T(8,128)} %fusion.39, f32[]{:T(128)} %bitcast.5, f32[]{:T(128)} %bitcast.4, pred[4096]{0:T(1024)(128)(4,1)S(1)} %get-tuple-element.21, f32[]{:T(128)} %bitcast.3, ...), kind=kLoop, calls=%fused_computation.68 | loop fusion | flops 113245184 | bytes 33570852 | tf_op jit(solution)/shard_map/reduce_max | solution.py:43
  166.2 8.1 %fusion.22 = f32[1024]{0:T(1024)S(1)} fusion(f32[1024,4096]{1,0:T(8,128)} %get-tuple-element.5, f32[1024]{0:T(1024)S(1)} %get-tuple-element.4), kind=kLoop, calls=%fused_computation.36 | loop fusion | flops 8387584 | bytes 16785408 | tf_op jit(solution)/shard_map/reduce_sum | solution.py:45
  174.3 8.8 %multiply_reduce_fusion = f32[1024]{0:T(1024)S(1)} fusion(f32[4096]{0:T(1024)S(1)} %get-tuple-element.24, f32[1024]{0:T(1024)S(1)} %bitcast.25, f32[4096]{0:T(1024)S(1)} %get-tuple-element.23, f32[1024]{0:T(1024)S(1)} %bitcast.23, f32[1024]{0:T(1024)S(1)} %fusion.22, f32[1024,4096]{1,0:T(8,128)} %get-tuple-element.5, f32[1024]{0:T(1024)S(1)} %get-tuple-element.4), kind=kLoop, calls=%fused_computation.20 | loop fusion | flops 29359104 | bytes 16830464 | tf_op jit(solution)/shard_map/reduce_sum | solution.py:47
  183.1 15.2 %broadcast_select_fusion.1 = (f32[1024,4096]{1,0:T(8,128)}, f32[1024,4096]{1,0:T(8,128)S(1)}) fusion(pred[4096]{0:T(1024)(128)(4,1)S(1)} %fusion.34, f32[1024]{0:T(1024)S(1)} %multiply_reduce_fusion, f32[4096]{0:T(1024)S(1)} %get-tuple-element.24, f32[1024]{0:T(1024)S(1)} %bitcast.26, f32[4096]{0:T(1024)S(1)} %get-tuple-element.23, f32[1024]{0:T(1024)S(1)} %bitcast.24, ...), kind=kLoop, calls=%fused_computation.38 | loop fusion | flops 33554432 | bytes 50388992 | tf_op jit(solution)/shard_map/jit(_where)/select_n | solution.py:52
  198.3 11.7 %broadcast_select_fusion = (f32[1024,4096]{1,0:T(8,128)}, f32[1024,4096]{1,0:T(8,128)}) fusion(f32[1024,4096]{1,0:T(8,128)S(1)} %get-tuple-element.3, pred[4096]{0:T(1024)(128)(4,1)S(1)} %get-tuple-element.21, pred[4096]{0:T(1024)(128)(4,1)S(1)} %get-tuple-element.22), kind=kLoop, calls=%fused_computation.37 | loop fusion | flops 8388608 | bytes 50339840 | tf_op jit(solution)/shard_map/jit(_where)/select_n | solution.py:52
  210.0 0.0 copy-start.2
  210.0 79.9 %fusion.9 = bf16[1024,4096]{1,0:T(8,128)(2,1)S(1)} fusion(f32[1024,4096]{1,0:T(8,128)} %get-tuple-element.9, f32[1024,4096]{1,0:T(8,128)} %get-tuple-element.8, f32[1024,4096]{1,0:T(8,128)} %get-tuple-element.2, f32[]{:T(128)} %bitcast.9, f32[]{:T(128)} %bitcast.8, f32[]{:T(128)} %bitcast.7, f32[]{:T(128)} %bitcast.6, f32[]{:T(128)} %bitcast.5, f32[]{:T(128)} %bitcast.4, ...), kind=kLoop, calls=%fused_computation.13 | loop fusion | flops 75497472 | bytes 58720292 | tf_op jit(solution)/shard_map/convert_element_type | solution.py:54
  290.0 0.0 copy-start.1
  290.0 3.2 copy-done.1
  293.2 3.3 fusion.37
  296.5 0.0 all-reduce.9.cloned.1.call-update
  296.5 0.0 reduce-scatter.2.cloned.1.call-start
  296.6 0.0 copy-done.2
  296.6 7.8 %fusion.44 = f32[4096,256]{1,0:T(8,128)} fusion(bf16[1024,4096]{1,0:T(8,128)(2,1)} %copy-done.1, bf16[1024,256]{1,0:T(8,128)(2,1)S(1)} %copy-done.2), kind=kOutput, calls=%fused_computation.71 | convolution fusion | flops 2147483648 | bytes 13107200 | tf_op jit(solution)/shard_map/dot_general | solution.py:57
  304.4 48.3 %all-reduce.9.cloned.1.call-done = f32[1024,256]{1,0:T(8,128)} async-done(((f32[1024,256]{1,0:T(8,128)}), f32[1024,256]{1,0:T(8,128)}) %all-reduce.9.cloned.1.call-update) | async-done | bytes 1048592 | tf_op jit(solution)/shard_map/psum | solution.py:60
  352.7 11.2 %scatter_custom_fusion = f32[4096,256]{1,0:T(8,128)} fusion(f32[4096,256]{1,0:T(8,128)} %fusion.44, s32[1024]{0:T(1024)S(1)} %get-tuple-element.7, f32[1024,256]{1,0:T(8,128)} %all-reduce.9.cloned.1.call-done, f32[]{:T(128)} %constant.51.clone.1, pred[1024]{0:T(1024)(128)(4,1)S(1)} %compare_and_fusion), kind=kCustom, calls=%fused_computation.40 | custom fusion | flops 524288 | bytes 5244416 | tf_op jit(solution)/shard_map/scatter-add | solution.py:65
  363.9 0.0 reduce-scatter.2.cloned.1.call-update
  364.0 76.2 %reduce-scatter.2.cloned.1.call-done = f32[1,1024,256]{2,1,0:T(8,128)} async-done(((f32[1,4096,256]{2,1,0:T(8,128)}), f32[1,1024,256]{2,1,0:T(8,128)}) %reduce-scatter.2.cloned.1.call-update) | async-done | bytes 1048592 | tf_op jit(solution)/shard_map/reduce_scatter | solution.py:68
  440.2 2.3 copy.10
  (3 shorter events, 0.0 us)
Async XLA Ops:
  7.2 1.6 copy-start
  7.2 64.2 %all-reduce.7.cloned.1.call-start = ((), (), s32[]{:S(2)}) async-start(), calls=%async_computation.1 | async-start | bytes 1048576 | tf_op jit(solution)/shard_map/psum | solution.py:24
  13.8 338.9 %all-reduce.9.cloned.1.call-start = ((), (), s32[]{:S(2)}) async-start(), calls=%async_computation.2 | async-start | bytes 2097152 | tf_op jit(solution)/shard_map/psum | solution.py:60
  210.0 86.6 %copy-start.2 = (bf16[1024,256]{1,0:T(8,128)(2,1)S(1)}, bf16[1024,256]{1,0:T(8,128)(2,1)}, u32[]{:S(2)}) copy-start(bf16[1024,256]{1,0:T(8,128)(2,1)} %all-reduce.7.cloned.1.call-done) | copy-start | bytes 1572868
  290.0 3.2 copy-start.1
  296.5 143.6 %reduce-scatter.2.cloned.1.call-start = ((), (), s32[]{:S(2)}) async-start(), calls=%async_computation.3 | async-start | bytes 5242880 | tf_op jit(solution)/shard_map/reduce_scatter | solution.py:68
Sparse Core Ops, SparseCore 0:
  13.9 57.4 all-reduce.6
  296.7 55.9 all-reduce.8
  364.1 76.0 reduce-scatter.1
where the time goes:
time: 450 us; the launch traced here: 449 us
  other arithmetic  223 us (50%)
  waiting for transfers between devices  180 us (40%)
  matrix products  20.3 us (5%)
  between operations  13.8 us (3%)
  local copies, waits for them, and re-layouts  11.8 us (3%)
    reduce_max x1, other arithmetic, shards(): top = jnp.max(logits, axis=1, keepdims=True)  85.7 us
    convert_element_type x1, other arithmetic, shards(): dcost = dcost.astype(jnp.bfloat16)  79.9 us
    reduce_scatter x1, waiting for transfers between devices, shards(): lax.psum_scatter(feature_term, 'query', scatter_dimension=1, tiled=True)  76.2 us
    psum x1, waiting for transfers between devices, shards(): qfeat = lax.psum(picked.astype(jnp.bfloat16), 'frame')  55.2 us
    psum x1, waiting for transfers between devices, shards(): query_grad = lax.psum(query_part, 'frame')  48.3 us
    select_n x2, other arithmetic, shards(): masked = jnp.where(col_masks[b], dlogit, 0.0)  26.9 us
    scatter-add x1, other arithmetic, shards(): feature_term = feature_term.reshape(t_dev * pixels, chan).at[flat_rows].a...  11.2 us
    dot_general x1, matrix products, shards(): lax.dot_general(qfeat, frame_map, (((1,), (1,)), ((), ())), preferred_ele...  9.14 us
  transfers between devices with their start and end apart: 3, of which 3 were waited for; matrix products, arithmetic and copies ran while one was open for 2% of the time, Pallas kernels for 0%

commit v1 on v0

v1 whole, which is shorter than its diff:
```python
import functools
import math

import jax
import jax.numpy as jnp
from jax import lax
from jax.experimental import pallas as pl
from jax.experimental.pallas import tpu as pltpu
from jax.sharding import PartitionSpec as P

W = 64
LOG2E = math.log2(math.e)
F32 = jnp.float32
BF16 = jnp.bfloat16
NT = (((1,), (1,)), ((), ()))


def dot(a, b):
    return jnp.dot(a, b, preferred_element_type=F32)


def conv_rows(pad_ref, weights, sign, first, count):
    chan = pad_ref.shape[1]
    col = lax.broadcasted_iota(jnp.int32, (W, chan), 0)
    keep_low, keep_high = col >= 1, col <= W - 2
    rows = [
        pad_ref[pl.ds(pl.multiple_of((first + r) * W, W), W), :] for r in range(count + 2)
    ]
    out = []
    for r in range(count):
        taps = {}
        for b in (-1, 0, 1):
            taps[b] = sum(
                weights[sign * a + 1][sign * b + 1] * rows[r + 1 + a] for a in (-1, 0, 1)
            )
        left = jnp.where(keep_low, pltpu.roll(taps[-1], 1, 0), 0.0)
        right = jnp.where(keep_high, pltpu.roll(taps[1], W - 1, 0), 0.0)
        out.append(taps[0] + left + right)
    return jnp.concatenate(out, axis=0)


def load_weights(k_ref):
    return [[k_ref[a, b] for b in range(3)] for a in range(3)]


def prep_kernel(k_ref, f_ref, gg_ref, th_ref, pad_ref):
    pixels, chan = f_ref.shape
    weights = load_weights(k_ref)
    zero = jnp.zeros((W, chan), F32)
    pad_ref[pl.ds(0, W), :] = zero
    pad_ref[pl.ds(pixels + W, W), :] = zero

    def widen(i, c):
        rows = pl.multiple_of(i * 256, 256)
        pad_ref[pl.ds(rows + W, 256), :] = f_ref[pl.ds(rows, 256), :].astype(F32)
        return c

    lax.fori_loop(0, pixels // 256, widen, 0)

    def step(i, c):
        g = conv_rows(pad_ref, weights, 1, i * 4, 4)
        scaled = g * LOG2E
        hi = scaled.astype(BF16)
        at = pl.ds(pl.multiple_of(i * 4 * W, 4 * W), 4 * W)
        gg_ref[at, pl.ds(0, chan)] = hi
        gg_ref[at, pl.ds(chan, chan)] = (scaled - hi.astype(F32)).astype(BF16)
        th_ref[:, at] = g.T.astype(BF16)
        return c

    lax.fori_loop(0, pixels // (4 * W), step, 0, unroll=4)


VMEM = pl.BlockSpec(memory_space=pltpu.VMEM)
SMEM = pl.BlockSpec(memory_space=pltpu.SMEM)


def prep(kernel, frame_map):
    pixels, chan = frame_map.shape
    return pl.pallas_call(
        prep_kernel,
        out_shape=(
            jax.ShapeDtypeStruct((pixels, 2 * chan), BF16),
            jax.ShapeDtypeStruct((chan, pixels), BF16),
        ),
        in_specs=[SMEM, VMEM],
        out_specs=(VMEM, VMEM),
        scratch_shapes=[pltpu.VMEM((pixels + 2 * W, chan), F32)],
        compiler_params=pltpu.CompilerParams(vmem_limit_bytes=12 << 20),
        cost_estimate=pl.CostEstimate(
            flops=40 * pixels * chan, bytes_accessed=10 * pixels * chan, transcendentals=0
        ),
        name="prep",
    )(kernel, frame_map)


def attend_kernel(zero_ref, q_ref, gy_ref, gx_ref, gg_ref, th_ref, *refs):
    (qg_ref, d_ref), scratch = refs[:2], refs[2:]
    pixels = gg_ref.shape[0]
    nb = scratch[0].shape[1]
    blocks = q_ref.shape[0] // nb
    height = pixels // W
    chunk = 4 * W
    steps = pixels // chunk
    mid = (height - 1) / 2.0
    rx = lax.broadcasted_iota(jnp.int32, (W, nb), 0).astype(F32) - (W - 1) / 2.0
    back = pl.multiple_of(zero_ref[0], W)
    maps, exp_ref = scratch[:-1], scratch[-1]

    def lanes(i):
        return pl.ds(i * nb, nb)

    def logits(i, c, m):
        at = pl.ds(c * chunk, chunk)
        q = q_ref[lanes(i), :]
        qq = jnp.concatenate([q, q], axis=1)
        l = lax.dot_general(gg_ref[at, :], qq, NT, preferred_element_type=F32)
        maps[i % len(maps)][at, :] = l
        return jnp.maximum(m, jnp.max(l.reshape(chunk // 8, 8, nb), axis=0))

    def exps(i, c, top, cols, ys):
        for h in range(c * chunk // W, (c + 1) * chunk // W):
            e = jnp.exp2(maps[i % len(maps)][pl.ds(back + h * W, W), :] - top)
            exp_ref[pl.ds(h * W, W), :] = e
            ys = ys + jnp.sum(e.reshape(W // 8, 8, nb), axis=0) * (h - mid)
            cols = cols + e
        return cols, ys

    def stats(i, cols, ys):
        total = jnp.sum(cols, axis=0, keepdims=True)
        ex = jnp.sum(cols * rx, axis=0, keepdims=True)
        ey = jnp.sum(ys, axis=0, keepdims=True)
        inv = 1.0 / total
        gy, gx = gy_ref[:, lanes(i)], gx_ref[:, lanes(i)]
        mean = (gy * ey + gx * ex) * inv
        return (gx * rx - mean) * inv, gy * inv

    low = jnp.full((8, nb), -jnp.inf, F32)
    m = low
    for c in range(steps):
        m = logits(0, c, m)
    for i in range(blocks):
        top = jnp.max(m, axis=0, keepdims=True)
        m, cols, ys = low, jnp.zeros((W, nb), F32), jnp.zeros((8, nb), F32)
        for c in range(steps):
            cols, ys = exps(i, c, top, cols, ys)
            if i + 1 < blocks:
                m = logits(i + 1, c, m)
        u, v = stats(i, cols, ys)
        grad = None
        for g in range(4):
            for h in range(g * height // 4, (g + 1) * height // 4):
                e = exp_ref[pl.ds(back + h * W, W), :]
                d_ref[pl.ds(h * W, W), lanes(i)] = (e * (u + v * (h - mid))).astype(BF16)
            at = pl.ds(g * pixels // 4, pixels // 4)
            part = dot(th_ref[:, at], d_ref[at, lanes(i)])
            grad = part if grad is None else grad + part
        qg_ref[lanes(i), :] = grad.T


def attend(zero, q, gy, gx, gg, th):
    nq, chan = q.shape
    pixels = gg.shape[0]
    nb = min(256, nq)
    return pl.pallas_call(
        attend_kernel,
        out_shape=(
            jax.ShapeDtypeStruct((nq, chan), F32),
            jax.ShapeDtypeStruct((pixels, nq), BF16),
        ),
        in_specs=[SMEM] + [VMEM] * 5,
        out_specs=(VMEM, VMEM),
        scratch_shapes=[pltpu.VMEM((pixels, nb), F32)] * (min(2, nq // nb) + 1),
        compiler_params=pltpu.CompilerParams(vmem_limit_bytes=20 << 20),
        cost_estimate=pl.CostEstimate(
            flops=6 * nq * pixels * chan,
            bytes_accessed=8 * pixels * chan,
            transcendentals=nq * pixels,
        ),
        name="attend",
    )(zero, q, gy, gx, gg, th)


def shard_at(where_ref, nz, hop):
    zi = where_ref[1]
    if hop is None:
        return zi
    level, j = hop
    return jnp.where(zi == nz - level, j, nz - 1 - j)


def feature_kernel(nz, plan, count_d, k_ref, where_ref, *refs):
    pairs = list(zip(refs[:count_d], refs[count_d : 2 * count_d]))
    outs, (y_ref, acc_ref) = refs[2 * count_d : -2], refs[-2:]
    pixels, chan = y_ref.shape
    weights = load_weights(k_ref)
    zero = jnp.zeros((W, chan), F32)
    acc_ref[pl.ds(0, W), :] = zero
    acc_ref[pl.ds(pixels + W, W), :] = zero
    count = 4
    steps = pixels // (count * W)
    ready = [0]

    def product(i):
        at = pl.ds(i * count * W, count * W)
        acc_ref[pl.ds(i * count * W + W, count * W), :] = sum(
            dot(d_ref[at, :], q_ref[...]) for d_ref, q_ref in pairs
        )

    def taps(upto):
        n = upto - ready[0]
        if n > 0:
            y_ref[pl.ds(ready[0] * W, n * W), :] = conv_rows(acc_ref, weights, -1, ready[0], n)
            ready[0] = upto

    for i in range(steps):
        product(i)
        if i > 0:
            taps(i * count - 1)
    taps(steps * count)
    shard = pixels // nz
    for out_ref, (hop, start) in zip(outs, plan):
        base = pl.multiple_of(shard_at(where_ref, nz, hop) * shard + start, 16)
        out_ref[...] = y_ref[pl.ds(base, out_ref.shape[0]), :].astype(out_ref.dtype)


def first_kernel(nz, count_d, k_ref, where_ref, *refs):
    pairs = list(zip(refs[:count_d], refs[count_d : 2 * count_d]))
    outs, (y_ref, acc_ref) = refs[2 * count_d : -2], refs[-2:]
    shard, _ = y_ref.shape
    weights = load_weights(k_ref)
    count = 4
    size = count * W
    top = 2 * where_ref[1] >= nz
    base = jnp.where(top, 0, (nz - 1) * shard)

    def product(start, size):
        at = pl.ds(pl.multiple_of(start, W), size)
        return sum(dot(d_ref[at, :], q_ref[...]) for d_ref, q_ref in pairs)

    edge = product(jnp.where(top, shard, base - W), W)
    acc_ref[pl.ds(0, W), :] = edge * jnp.where(top, 0.0, 1.0)
    acc_ref[pl.ds(shard + W, W), :] = edge * jnp.where(top, 1.0, 0.0)
    done = 0
    for i in range(shard // size):
        acc_ref[pl.ds(i * size + W, size), :] = product(base + i * size, size)
        upto = (i + 1) * count - (1 if (i + 1) * size < shard else 0)
        y_ref[pl.ds(done * W, (upto - done) * W), :] = conv_rows(
            acc_ref, weights, -1, done, upto - done
        )
        done = upto
    start = 0
    for out_ref in outs:
        part = out_ref.shape[0]
        out_ref[...] = y_ref[pl.ds(start, part), :].astype(out_ref.dtype)
        start = (start + part) % shard


def first_terms(kernel, where, nz, cut, ds, qs):
    pixels, chan = ds[0].shape[0], qs[0].shape[1]
    nq = sum(q.shape[0] for q in qs)
    shard = pixels // nz
    sizes = (cut, shard - cut)
    return pl.pallas_call(
        functools.partial(first_kernel, nz, len(ds)),
        out_shape=tuple(
            jax.ShapeDtypeStruct((size, chan), kind) for kind in (BF16, F32) for size in sizes
        ),
        in_specs=[SMEM, SMEM] + [VMEM] * (2 * len(ds)),
        out_specs=(VMEM,) * 4,
        scratch_shapes=[
            pltpu.VMEM((shard, chan), F32),
            pltpu.VMEM((shard + 2 * W, chan), F32),
        ],
        compiler_params=pltpu.CompilerParams(vmem_limit_bytes=8 << 20),
        cost_estimate=pl.CostEstimate(
            flops=2 * nq * shard * chan, bytes_accessed=8 * shard * chan, transcendentals=0
        ),
        name="first",
    )(kernel, where, *ds, *qs)


def feature_terms(kernel, where, nz, hops, ds, qs):
    pixels, chan = ds[0].shape[0], qs[0].shape[1]
    nq = sum(q.shape[0] for q in qs)
    plan = [((level, j), start) for level, j, _, start, _ in hops] + [(None, 0)]
    shapes = [(size, BF16 if level == 1 else F32) for level, _, _, _, size in hops]
    shapes.append((pixels // nz, F32))
    return pl.pallas_call(
        functools.partial(feature_kernel, nz, plan, len(ds)),
        out_shape=tuple(jax.ShapeDtypeStruct((size, chan), kind) for size, kind in shapes),
        in_specs=[SMEM, SMEM] + [VMEM] * (2 * len(ds)),
        out_specs=(VMEM,) * len(shapes),
        scratch_shapes=[
            pltpu.VMEM((pixels, chan), F32),
            pltpu.VMEM((pixels + 2 * W, chan), F32),
        ],
        compiler_params=pltpu.CompilerParams(vmem_limit_bytes=14 << 20),
        cost_estimate=pl.CostEstimate(
            flops=2 * nq * pixels * chan, bytes_accessed=8 * pixels * chan, transcendentals=0
        ),
        name="feature",
    )(kernel, where, *ds, *qs)


def place_kernel(nz, odd, where_ref, *refs):
    ids_refs, rows_ref = refs[:nz], refs[nz]
    half, blocks, rows, chan = rows_ref.shape
    near_ref = refs[nz + 1] if odd else None
    so_far_ref = refs[nz + 2] if odd else None
    out_ref = refs[nz + 3] if odd else refs[nz + 1]
    shard = out_ref.shape[0]
    me, first = where_ref[0], where_ref[2]
    ids = []
    for i in range(half):
        owner = pl.ds(me ^ (2 * i + odd), 1)
        own = ids_refs[0][owner, :]
        ids.append(jnp.concatenate([own, own] + [r[owner, :] for r in ids_refs[1:]], axis=1) - first)
    size = min(256, shard)
    for b in range(shard // size):
        at = pl.ds(b * size, size)
        total = so_far_ref[at, :] if odd else jnp.zeros((size, chan), F32)
        for i in range(half):
            pix = lax.broadcasted_iota(jnp.int32, (size, blocks * rows), 0) + b * size
            hit = jnp.where(pix == ids[i], 1.0, 0.0).astype(BF16)
            total += dot(hit, rows_ref[i].reshape(blocks * rows, chan))
        out_ref[at, :] = total
    if odd:
        grad_ref = refs[nz + 4]
        for i in range(half):
            for k, ref in ((2 * i, near_ref), (2 * i + 1, rows_ref)):
                at = pl.ds(pl.multiple_of((me ^ k) * rows, rows), rows)
                grad_ref[at, :] = ref[i, 0].astype(F32) + ref[i, 1].astype(F32)


def place(where, ids, shard, rows, near=None, so_far=None):
    odd = near is not None
    half, blocks, count, chan = rows.shape
    total = jax.ShapeDtypeStruct((shard, chan), F32)
    grad = jax.ShapeDtypeStruct((2 * half * count, chan), F32)
    args = [where, *ids, rows] + ([near, so_far] if odd else [])
    return pl.pallas_call(
        functools.partial(place_kernel, len(ids), int(odd)),
        out_shape=(total, grad) if odd else total,
        in_specs=[SMEM] + [VMEM] * (len(args) - 1),
        out_specs=(VMEM, VMEM) if odd else VMEM,
        compiler_params=pltpu.CompilerParams(vmem_limit_bytes=12 << 20),
        cost_estimate=pl.CostEstimate(
            flops=2 * half * blocks * count * shard * chan,
            bytes_accessed=4 * shard * chan,
            transcendentals=0,
        ),
        name="place",
    )(*args)


def shards(nf, nz, features, kernel, cotangent, query_frame, query_pixel):
    _, pixels, chan = features.shape
    nq = query_frame.shape[0]
    half = nf // 2
    rows = nq // nf
    shard = pixels // nz
    me = lax.axis_index("frame")
    zi = lax.axis_index("query")
    frame_map = features[0]

    def fx(v, k):
        return lax.ppermute(v, "frame", [(i, i ^ k) for i in range(nf)])

    def zx(v, k):
        return lax.ppermute(v, "query", [(i, i ^ k) for i in range(nz)])

    def swap(v):
        lead = v.shape[:-2]
        bit = 1
        while bit < nf:
            w = v.reshape(*lead, nf // (2 * bit), 2, bit, rows)
            turned = jnp.concatenate([w[..., 1:, :, :], w[..., :1, :, :]], axis=-3)
            v = jnp.where((me & bit) != 0, turned, w).reshape(*lead, nf, rows)
            bit *= 2
        return v

    def relative(v):
        lead = v.shape[:-1]
        v = swap(v.reshape(*lead, nf, rows))
        v = v.reshape(*lead, half, 2, rows)
        return jnp.swapaxes(v, -3, -2).reshape(*lead, nf, rows)

    flat = query_frame * pixels + query_pixel
    local = relative(flat - me * pixels).reshape(-1)
    owned = (local >= 0) & (local < pixels)
    picked = frame_map[jnp.clip(local, 0, pixels - 1)]
    picked = jnp.where(owned[:, None], picked, jnp.zeros((), BF16))
    picked = picked.reshape(nf, rows, chan)
    near, far = nq // 2, nq - nq // 2
    pulls = relative(cotangent[:, 0, :]).reshape(2, nq)
    cuts = [(near, nq), (0, near)]
    pulls = [[pulls[:1, a:b], pulls[1:, a:b]] for a, b in cuts]
    zero = jnp.minimum(zi, 0).astype(jnp.int32)[None]
    where = jnp.stack([me, zi, me * pixels + zi * shard]).astype(jnp.int32)
    flat = flat.reshape(nf, rows)
    frame_map, pulls, where, zero, flat = lax.optimization_barrier(
        (frame_map, pulls, where, zero, flat)
    )
    gg, th = prep(kernel, frame_map)

    mine = picked[:half] + fx(picked[half:], 1)
    mine, flat = lax.optimization_barrier((mine, flat))
    others = [zx(flat, k) for k in range(1, nz)]
    own = mine[0]
    for i in range(1, half):
        own = own + fx(mine[i], 2 * i)
    same = jnp.stack([own] + [fx(own, 2 * i) for i in range(1, half)])
    other = fx(same, 1)
    same, other = same.reshape(near, chan), other.reshape(far, chan)

    far_part, far_d = attend(zero, other, *pulls[0], gg, th)
    crossed = fx(far_part, 1)
    near_part, near_d = attend(zero, same, *pulls[1], gg, th)
    hops = []
    for level in range(1, nz):
        for j in range(nz - level):
            cut = max(16, shard // 2 - 16 * (1 + j % 4))
            if level == 1 and j == nz - 2:
                hops.append((level, j, 0, 0, shard))
            else:
                hops += [(level, j, 0, 0, cut), (level, j, 1, cut, shard - cut)]
    hops.sort(key=lambda h: (h[0] > 1, h[0] + 1.9 * h[1] + 1.1 * h[2]))
    ds, qs = [far_d, near_d], [other, same]
    terms = {}
    firsts = first_terms(kernel, where, nz, hops[0][4], ds, qs)
    terms[1, 0, 0], terms[1, 0, 1], terms[2, 0, 0], terms[2, 0, 1] = firsts
    rest = [h for h in hops if h[:3] not in terms]
    results = feature_terms(kernel, where, nz, rest, ds, qs)
    terms.update({h[:3]: v for h, v in zip(rest, results)})
    came = {}
    for level, j, p, _, _ in hops:
        v = terms[level, j, p]
        if level > 1:
            v = (v + came[level - 1, j, p].astype(F32)).astype(BF16)
        hop = [(nz - level, nz - level - 1), (level - 1, level)]
        came[level, j, p] = lax.ppermute(v, "query", hop)
    arrived = sum(
        jnp.concatenate(
            [came[h[:3]] for h in sorted(hops) if h[0] == level and h[1] == nz - level - 1]
        ).astype(F32)
        for level in range(1, nz)
    )

    mine = (near_part + crossed).reshape(half, rows, chan)
    own = mine[0]
    for i in range(1, half):
        own = own + fx(mine[i], 2 * i)
    upper = own.astype(BF16)
    lower = (own - upper.astype(F32)).astype(BF16)
    known = jnp.stack([upper, lower] + [zx(upper, k) for k in range(1, nz)])
    near = jnp.stack([known] + [fx(known, 2 * i) for i in range(1, half)])
    far = fx(near, 1)
    ids = [flat] + others
    placed = place(where, ids, shard, near)
    placed, query_grad = place(where, ids, shard, far, near, placed)
    feature_grad = results[-1] + arrived + placed
    return query_grad, feature_grad[None]


def solution(mesh):
    nf, nz = mesh.shape["frame"], mesh.shape["query"]
    placed = (P("frame", None, None), P(), P(None, "frame", "query"), P("query"), P("query"))

    def body(*args):
        return shards(nf, nz, *args)

    return jax.shard_map(
        body,
        mesh=mesh,
        in_specs=placed,
        out_specs=(P("query", None), P("frame", "query", None)),
        check_vma=False,
    )
```

time: 450 us -> 115 us (0.26)
  other arithmetic: 223 us -> 3.17 us
  waiting for transfers between devices: 180 us -> 28.1 us
  starting transfers between devices: 0.12 us -> 47.8 us
  Pallas kernels: 0 us -> 29.1 us
  matrix products: 20.3 us -> 0 us
  between operations: 13.8 us -> 1.22 us
  local copies, waits for them, and re-layouts: 11.8 us -> 5.52 us
    psum x2 -> x0, waiting for transfers between devices: 103 us -> none  [the longest x1 55.2 us: shards(): qfeat = lax.psum(picked.astype(jnp.bfloat16), 'frame')]
    reduce_max x1 -> x0, other arithmetic: 85.7 us -> none  [shards(): top = jnp.max(logits, axis=1, keepdims=True)]
    convert_element_type x1 -> x6, other arithmetic: 79.9 us -> 0.41 us  [shards(): v = (v + came[level - 1, j, p].astype(F32)).astype(BF16)]
    reduce_scatter x1 -> x0, waiting for transfers between devices: 76.2 us -> none  [shards(): lax.psum_scatter(feature_term, 'query', scatter_dimension=1, tiled=True)]
    ppermute x0 -> x33, starting transfers between devices: none -> 47.8 us  [the longest x11 24.4 us: shards(): came[level, j, p] = lax.ppermute(v, 'query', hop)]
    pallas_call x0 -> x7, Pallas kernels: none -> 29.1 us  [the longest x2 9.77 us: attend(): pl.pallas_call(attend_kernel, out_shape=(jax.ShapeDtypeStruct((nq, chan),...]
    ppermute x0 -> x33, waiting for transfers between devices: none -> 28.1 us  [the longest x16 14.7 us: fx(): return lax.ppermute(v, 'frame', [(i, i ^ k) for i in range(nf)])]
    select_n x3 -> x4, other arithmetic: 27.9 us -> 0.22 us  [the longest x1 0.2 us: shards(): picked = jnp.where(owned[:, None], picked, jnp.zeros((), BF16))]
  transfers between devices with their start and end apart: 3 -> 33, of which waited for: 3 -> 15; matrix products, arithmetic and copies ran while one was open for 2% -> 1% of each run, Pallas kernels for 0% -> 21%
where the time goes in v1:
time: 115 us
  starting transfers between devices  47.8 us (42%)
  Pallas kernels  29.1 us (25%)
  waiting for transfers between devices  28.1 us (24%)
  local copies, waits for them, and re-layouts  5.52 us (5%)
  other arithmetic  3.17 us (3%)
  between operations  1.22 us (1%)
    ppermute x11, starting transfers between devices, shards(): came[level, j, p] = lax.ppermute(v, 'query', hop)  24.4 us
    ppermute x16, starting transfers between devices, fx(): return lax.ppermute(v, 'frame', [(i, i ^ k) for i in range(nf)])  16.3 us
    ppermute x16, waiting for transfers between devices, fx(): return lax.ppermute(v, 'frame', [(i, i ^ k) for i in range(nf)])  14.7 us
    pallas_call x2, Pallas kernels, attend(): pl.pallas_call(attend_kernel, out_shape=(jax.ShapeDtypeStruct((nq, chan),...  9.77 us
    ppermute x11, waiting for transfers between devices, shards(): came[level, j, p] = lax.ppermute(v, 'query', hop)  7.55 us
    ppermute x6, starting transfers between devices, zx(): return lax.ppermute(v, 'query', [(i, i ^ k) for i in range(nz)])  7.12 us
    pallas_call x1, Pallas kernels, feature_terms(): pl.pallas_call(functools.partial(feature_kernel, nz, plan, len(ds)), out_...  6.46 us
    ppermute x6, waiting for transfers between devices, zx(): return lax.ppermute(v, 'query', [(i, i ^ k) for i in range(nz)])  5.82 us
  transfers between devices with their start and end apart: 33, of which 15 were waited for; matrix products, arithmetic and copies ran while one was open for 1% of the time, Pallas kernels for 21%

profile of v1, /device:TPU:0, one launch (start us, length us, event | category | flops | bytes accessed | tf_op | source)
XLA Modules:
  0.0 115.0 jit_solution(9935169454965650183)
XLA Ops:
  0.6 0.7 broadcast_subtract_fusion
  1.5 5.3 %gather_fusion = bf16[1024,256]{1,0:T(8,128)(2,1)S(1)} fusion(bf16[4096,256]{1,0:T(8,128)(2,1)} %bitcast.96, s32[1024]{0:T(1024)S(1)} %broadcast_clamp_fusion), kind=kCustom, calls=%fused_computation | custom fusion | bytes 1052672 | tf_op jit(solution)/shard_map/gather | solution.py:391
  7.1 0.6 collective-permute-start
  8.0 0.9 collective-permute-done
  8.9 2.9 %collective-permute-start.4 = (bf16[128,256]{1,0:T(8,128)(2,1)S(1)}, bf16[128,256]{1,0:T(8,128)(2,1)S(1)}, u32[]{:S(2)}, u32[]{:S(2)}) collective-permute-start(bf16[128,256]{1,0:T(8,128)(2,1)S(1)} %get-tuple-element.72), channel_id=1, source_target_pairs={{0,8},{4,12},{8,0},{12,4},{16,24},{20,28},{24,16},{28,20},{1,9},{5... | collective-permute-start | bytes 196616 | tf_op jit(solution)/shard_map/ppermute | solution.py:367
  11.9 1.5 %collective-permute-start.5 = (bf16[128,256]{1,0:T(8,128)(2,1)S(1)}, bf16[128,256]{1,0:T(8,128)(2,1)S(1)}, u32[]{:S(2)}, u32[]{:S(2)}) collective-permute-start(bf16[128,256]{1,0:T(8,128)(2,1)S(1)} %get-tuple-element.74), channel_id=1, source_target_pairs={{0,16},{4,20},{8,24},{12,28},{16,0},{20,4},{24,8},{28,12},{1,17},{... | collective-permute-start | bytes 196616 | tf_op jit(solution)/shard_map/ppermute | solution.py:367
  13.4 0.9 collective-permute-done.4
  14.2 1.9 %collective-permute-done.5 = bf16[128,256]{1,0:T(8,128)(2,1)S(1)} collective-permute-done((bf16[128,256]{1,0:T(8,128)(2,1)S(1)}, bf16[128,256]{1,0:T(8,128)(2,1)S(1)}, u32[]{:S(2)}, u32[]{:S(2)}) %collective-permute-start.5) | collective-permute-done | bytes 65568 | tf_op jit(solution)/shard_map/ppermute | solution.py:367
  16.1 2.4 %collective-permute-done.6 = bf16[128,256]{1,0:T(8,128)(2,1)S(1)} collective-permute-done((bf16[128,256]{1,0:T(8,128)(2,1)S(1)}, bf16[128,256]{1,0:T(8,128)(2,1)S(1)}, u32[]{:S(2)}, u32[]{:S(2)}) %collective-permute-start.6) | collective-permute-done | bytes 65568 | tf_op jit(solution)/shard_map/ppermute | solution.py:367
  18.6 0.6 collective-permute-start.7
  19.6 2.5 %collective-permute-start.9 = (bf16[128,256]{1,0:T(8,128)(2,1)S(1)}, bf16[128,256]{1,0:T(8,128)(2,1)S(1)}, u32[]{:S(2)}, u32[]{:S(2)}) collective-permute-start(bf16[128,256]{1,0:T(8,128)(2,1)S(1)} %fusion.5), channel_id=1, source_target_pairs={{0,24},{4,28},{8,16},{12,20},{16,8},{20,12},{24,0},{28,4},{1,25},{... | collective-permute-start | bytes 196616 | tf_op jit(solution)/shard_map/ppermute | solution.py:367
  22.1 0.8 collective-permute-done.7
  23.4 1.3 %collective-permute-done.9 = bf16[128,256]{1,0:T(8,128)(2,1)S(1)} collective-permute-done((bf16[128,256]{1,0:T(8,128)(2,1)S(1)}, bf16[128,256]{1,0:T(8,128)(2,1)S(1)}, u32[]{:S(2)}, u32[]{:S(2)}) %collective-permute-start.9) | collective-permute-done | bytes 65568 | tf_op jit(solution)/shard_map/ppermute | solution.py:367
  24.9 5.3 %prep.1 = (bf16[4096,512]{1,0:T(8,128)(2,1)S(1)}, bf16[256,4096]{1,0:T(8,128)(2,1)S(1)}) custom-call(f32[3,3]{1,0:T(4,128)S(1)} %copy-done.1, bf16[4096,256]{1,0:T(8,128)(2,1)S(1)} %bitcast.97), custom_call_target="tpu_custom_call" | custom-call | flops 41943040 | bytes 10485760 | tf_op jit(solution)/shard_map/prep/pallas_call | solution.py:79
  30.2 4.9 %attend.3 = (f32[512,256]{1,0:T(8,128)S(1)}, bf16[4096,512]{1,0:T(8,128)(2,1)S(1)}) custom-call(s32[1]{0:T(128)} %bitcast.17.zero_ref, bf16[512,256]{1,0:T(8,128)(2,1)S(1)} %bitcast.101, f32[1,512]{1,0:T(1,128)S(1)} %get-tuple-element.43.gy_ref, f32[1,512]{1,0:T(1,128)S(1)} %get-tuple-element.44.gx_ref, bf16[4096,512]{1,0:T(8,128)(2,1)S(1)} %get-tuple-element.40.gg_ref, ...), custom_call_target="tpu_custom_call" | custom-call | flops 3221225472 | bytes 8388608 | tf_op jit(solution)/shard_map/attend/pallas_call | solution.py:164
  35.1 0.6 collective-permute-start.11
  35.6 4.9 %attend.2 = (f32[512,256]{1,0:T(8,128)S(1)}, bf16[4096,512]{1,0:T(8,128)(2,1)S(1)}) custom-call(s32[1]{0:T(128)} %bitcast.17.zero_ref, bf16[512,256]{1,0:T(8,128)(2,1)S(1)} %bitcast.98, f32[1,512]{1,0:T(1,128)S(1)} %get-tuple-element.37.gy_ref, f32[1,512]{1,0:T(1,128)S(1)} %get-tuple-element.38.gx_ref, bf16[4096,512]{1,0:T(8,128)(2,1)S(1)} %get-tuple-element.40.gg_ref, ...), custom_call_target="tpu_custom_call" | custom-call | flops 3221225472 | bytes 8388608 | tf_op jit(solution)/shard_map/attend/pallas_call | solution.py:164
  40.6 1.6 %collective-permute-start.12 = (f32[128,256]{1,0:T(8,128)S(1)}, f32[128,256]{1,0:T(8,128)S(1)}, u32[]{:S(2)}, u32[]{:S(2)}) collective-permute-start(f32[128,256]{1,0:T(8,128)S(1)} %get-tuple-element.67), channel_id=1, source_target_pairs={{0,8},{4,12},{8,0},{12,4},{16,24},{20,28},{24,16},{28,20},{1,9},{5... | collective-permute-start | bytes 393224 | tf_op jit(solution)/shard_map/ppermute | solution.py:367
  42.3 1.5 %collective-permute-start.13 = (f32[128,256]{1,0:T(8,128)S(1)}, f32[128,256]{1,0:T(8,128)S(1)}, u32[]{:S(2)}, u32[]{:S(2)}) collective-permute-start(f32[128,256]{1,0:T(8,128)S(1)} %get-tuple-element.69), channel_id=1, source_target_pairs={{0,16},{4,20},{8,24},{12,28},{16,0},{20,4},{24,8},{28,12},{1,17},{... | collective-permute-start | bytes 393224 | tf_op jit(solution)/shard_map/ppermute | solution.py:367
  44.2 2.3 %collective-permute-done.12 = f32[128,256]{1,0:T(8,128)S(1)} collective-permute-done((f32[128,256]{1,0:T(8,128)S(1)}, f32[128,256]{1,0:T(8,128)S(1)}, u32[]{:S(2)}, u32[]{:S(2)}) %collective-permute-start.12) | collective-permute-done | bytes 131104 | tf_op jit(solution)/shard_map/ppermute | solution.py:367
  46.5 3.8 %collective-permute-done.13 = f32[128,256]{1,0:T(8,128)S(1)} collective-permute-done((f32[128,256]{1,0:T(8,128)S(1)}, f32[128,256]{1,0:T(8,128)S(1)}, u32[]{:S(2)}, u32[]{:S(2)}) %collective-permute-start.13) | collective-permute-done | bytes 131104 | tf_op jit(solution)/shard_map/ppermute | solution.py:367
  50.3 1.6 %collective-permute-start.15 = (bf16[128,256]{1,0:T(8,128)(2,1)S(1)}, bf16[128,256]{1,0:T(8,128)(2,1)S(1)}, u32[]{:S(2)}, u32[]{:S(2)}) collective-permute-start(bf16[128,256]{1,0:T(8,128)(2,1)S(1)} %get-tuple-element.63), channel_id=1, source_target_pairs={{0,1},{1,0},{2,3},{3,2},{4,5},{5,4},{6,7},{7,6},{8,9},{9,8},{10,11... | collective-permute-start | bytes 196616 | tf_op jit(solution)/shard_map/ppermute | solution.py:370
  51.9 2.6 %collective-permute-start.16 = (bf16[128,256]{1,0:T(8,128)(2,1)S(1)}, bf16[128,256]{1,0:T(8,128)(2,1)S(1)}, u32[]{:S(2)}, u32[]{:S(2)}) collective-permute-start(bf16[128,256]{1,0:T(8,128)(2,1)S(1)} %get-tuple-element.63), channel_id=1, source_target_pairs={{0,2},{1,3},{2,0},{3,1},{4,6},{5,7},{6,4},{7,5},{8,10},{9,11},{10,... | collective-permute-start | bytes 196616 | tf_op jit(solution)/shard_map/ppermute | solution.py:370
  55.2 3.3 %collective-permute-done.16 = bf16[128,256]{1,0:T(8,128)(2,1)S(1)} collective-permute-done((bf16[128,256]{1,0:T(8,128)(2,1)S(1)}, bf16[128,256]{1,0:T(8,128)(2,1)S(1)}, u32[]{:S(2)}, u32[]{:S(2)}) %collective-permute-start.16) | collective-permute-done | bytes 65568 | tf_op jit(solution)/shard_map/ppermute | solution.py:370
  58.5 2.1 %collective-permute-done.17 = bf16[128,256]{1,0:T(8,128)(2,1)S(1)} collective-permute-done((bf16[128,256]{1,0:T(8,128)(2,1)S(1)}, bf16[128,256]{1,0:T(8,128)(2,1)S(1)}, u32[]{:S(2)}, u32[]{:S(2)}) %collective-permute-start.17) | collective-permute-done | bytes 65568 | tf_op jit(solution)/shard_map/ppermute | solution.py:370
  60.6 1.2 %collective-permute-start.18 = (bf16[5,128,256]{2,1,0:T(8,128)(2,1)S(1)}, bf16[5,128,256]{2,1,0:T(8,128)(2,1)S(1)}, u32[]{:S(2)}, u32[]{:S(2)}) collective-permute-start(bf16[5,128,256]{2,1,0:T(8,128)(2,1)S(1)} %bitcast_dynamic-update-slice_fusion), channel_id=1, source_target_pairs={{0,8},{4,12},{8,0},{12,4},{16,24},{20,28},{24,16},{28,20},{1,9},{5... | collective-permute-start | bytes 983048 | tf_op jit(solution)/shard_map/ppermute | solution.py:367
  61.8 0.8 collective-permute-start.19
  62.6 1.4 %collective-permute-start.20 = (bf16[5,128,256]{2,1,0:T(8,128)(2,1)S(1)}, bf16[5,128,256]{2,1,0:T(8,128)(2,1)S(1)}, u32[]{:S(2)}, u32[]{:S(2)}) collective-permute-start(bf16[5,128,256]{2,1,0:T(8,128)(2,1)S(1)} %bitcast_dynamic-update-slice_fusion), channel_id=1, source_target_pairs={{0,24},{4,28},{8,16},{12,20},{16,8},{20,12},{24,0},{28,4},{1,25},{... | collective-permute-start | bytes 983048 | tf_op jit(solution)/shard_map/ppermute | solution.py:367
  64.1 2.0 %first.1 = (bf16[496,256]{1,0:T(8,128)(2,1)S(1)}, bf16[528,256]{1,0:T(8,128)(2,1)S(1)}, f32[496,256]{1,0:T(8,128)S(1)}, f32[528,256]{1,0:T(8,128)S(1)}) custom-call(f32[3,3]{1,0:T(4,128)S(1)} %copy-done.1, s32[3]{0:T(128)S(1)} %pad_add_fusion.3.where_ref, bf16[4096,512]{1,0:T(8,128)(2,1)S(1)} %get-tuple-element.47.refs_0_, ...), custom_call_target="tpu_custom_call" | custom-call | flops 536870912 | bytes 2097152 | tf_op jit(solution)/shard_map/first/pallas_call | solution.py:263
  66.0 4.2 %collective-permute-start.27 = (bf16[496,256]{1,0:T(8,128)(2,1)S(1)}, bf16[496,256]{1,0:T(8,128)(2,1)S(1)}, u32[]{:S(2)}, u32[]{:S(2)}) collective-permute-start(bf16[496,256]{1,0:T(8,128)(2,1)S(1)} %get-tuple-element.57), channel_id=1, source_target_pairs={{3,2},{0,1},{7,6},{4,5},{11,10},{8,9},{15,14},{12,13},{19,18},{16,... | collective-permute-start | bytes 761864 | tf_op jit(solution)/shard_map/ppermute | solution.py:441
  70.2 6.5 %feature.1 = (bf16[480,256]{1,0:T(8,128)(2,1)S(1)}, bf16[544,256]{1,0:T(8,128)(2,1)S(1)}, bf16[1024,256]{1,0:T(8,128)(2,1)S(1)}, f32[496,256]{1,0:T(8,128)S(1)},...) custom-call(f32[3,3]{1,0:T(4,128)S(1)} %copy-done.1, ...), custom_call_target="tpu_custom_call" | custom-call | flops 2147483648 | bytes 8388608 | tf_op jit(solution)/shard_map/feature/pallas_call | solution.py:288
  76.8 3.5 %collective-permute-start.30 = (bf16[528,256]{1,0:T(8,128)(2,1)S(1)}, bf16[528,256]{1,0:T(8,128)(2,1)S(1)}, u32[]{:S(2)}, u32[]{:S(2)}) collective-permute-start(bf16[528,256]{1,0:T(8,128)(2,1)S(1)} %get-tuple-element.60), channel_id=1, source_target_pairs={{3,2},{0,1},{7,6},{4,5},{11,10},{8,9},{15,14},{12,13},{19,18},{16,... | collective-permute-start | bytes 811016 | tf_op jit(solution)/shard_map/ppermute | solution.py:441
  80.3 1.3 %collective-permute-start.25 = (bf16[544,256]{1,0:T(8,128)(2,1)S(1)}, bf16[544,256]{1,0:T(8,128)(2,1)S(1)}, u32[]{:S(2)}, u32[]{:S(2)}) collective-permute-start(bf16[544,256]{1,0:T(8,128)(2,1)S(1)} %get-tuple-element.54), channel_id=1, source_target_pairs={{3,2},{0,1},{7,6},{4,5},{11,10},{8,9},{15,14},{12,13},{19,18},{16,... | collective-permute-start | bytes 835592 | tf_op jit(solution)/shard_map/ppermute | solution.py:441
  81.9 3.2 %collective-permute-done.30 = bf16[528,256]{1,0:T(8,128)(2,1)S(1)} collective-permute-done((bf16[528,256]{1,0:T(8,128)(2,1)S(1)}, bf16[528,256]{1,0:T(8,128)(2,1)S(1)}, u32[]{:S(2)}, u32[]{:S(2)}) %collective-permute-start.30) | collective-permute-done | bytes 270368 | tf_op jit(solution)/shard_map/ppermute | solution.py:441
  85.1 0.7 collective-permute-start.28
  85.9 2.3 %collective-permute-done.25 = bf16[544,256]{1,0:T(8,128)(2,1)S(1)} collective-permute-done((bf16[544,256]{1,0:T(8,128)(2,1)S(1)}, bf16[544,256]{1,0:T(8,128)(2,1)S(1)}, u32[]{:S(2)}, u32[]{:S(2)}) %collective-permute-start.25) | collective-permute-done | bytes 278560 | tf_op jit(solution)/shard_map/ppermute | solution.py:441
  88.2 0.7 collective-permute-start.31
  88.9 2.6 %collective-permute-start.3 = (s32[8,128]{1,0:T(8,128)S(1)}, s32[8,128]{1,0:T(8,128)S(1)}, u32[]{:S(2)}, u32[]{:S(2)}) collective-permute-start(s32[8,128]{1,0:T(8,128)S(1)} %get-tuple-element.34.refs_0_), channel_id=1, source_target_pairs={{0,3},{1,2},{2,1},{3,0},{4,7},{5,6},{6,5},{7,4},{8,11},{9,10},{10,... | collective-permute-start | bytes 12296 | tf_op jit(solution)/shard_map/ppermute | solution.py:370
  91.6 7.9 %collective-permute-start.23 = (bf16[480,256]{1,0:T(8,128)(2,1)S(1)}, bf16[480,256]{1,0:T(8,128)(2,1)S(1)}, u32[]{:S(2)}, u32[]{:S(2)}) collective-permute-start(bf16[480,256]{1,0:T(8,128)(2,1)S(1)} %get-tuple-element.52), channel_id=1, source_target_pairs={{3,2},{0,1},{7,6},{4,5},{11,10},{8,9},{15,14},{12,13},{19,18},{16,... | collective-permute-start | bytes 737288 | tf_op jit(solution)/shard_map/ppermute | solution.py:441
  99.5 2.4 %collective-permute-start.22 = (bf16[1024,256]{1,0:T(8,128)(2,1)S(1)}, bf16[1024,256]{1,0:T(8,128)(2,1)S(1)}, u32[]{:S(2)}, u32[]{:S(2)}) collective-permute-start(bf16[1024,256]{1,0:T(8,128)(2,1)S(1)} %get-tuple-element.50), channel_id=1, source_target_pairs={{3,2},{0,1},{7,6},{4,5},{11,10},{8,9},{15,14},{12,13},{19,18},{16,... | collective-permute-start | bytes 1572872 | tf_op jit(solution)/shard_map/ppermute | solution.py:441
  101.9 0.7 collective-permute-start.26
  102.6 1.3 %collective-permute-start.29 = (bf16[496,256]{1,0:T(8,128)(2,1)S(1)}, bf16[496,256]{1,0:T(8,128)(2,1)S(1)}, u32[]{:S(2)}, u32[]{:S(2)}) collective-permute-start(bf16[496,256]{1,0:T(8,128)(2,1)S(1)} %add_convert_fusion.3), channel_id=1, source_target_pairs={{1,0},{2,3},{5,4},{6,7},{9,8},{10,11},{13,12},{14,15},{17,16},{18,... | collective-permute-start | bytes 761864 | tf_op jit(solution)/shard_map/ppermute | solution.py:441
  104.0 1.3 %collective-permute-start.32 = (bf16[528,256]{1,0:T(8,128)(2,1)S(1)}, bf16[528,256]{1,0:T(8,128)(2,1)S(1)}, u32[]{:S(2)}, u32[]{:S(2)}) collective-permute-start(bf16[528,256]{1,0:T(8,128)(2,1)S(1)} %add_convert_fusion.1), channel_id=1, source_target_pairs={{1,0},{2,3},{5,4},{6,7},{9,8},{10,11},{13,12},{14,15},{17,16},{18,... | collective-permute-start | bytes 811016 | tf_op jit(solution)/shard_map/ppermute | solution.py:441
  105.3 0.7 collective-permute-start.24
  106.0 2.3 %place.2.refs_6_ = f32[1024,256]{1,0:T(8,128)S(1)} custom-call(s32[3]{0:T(128)S(1)} %pad_add_fusion.3.where_ref, s32[8,128]{1,0:T(8,128)S(1)} %get-tuple-element.34.refs_0_, s32[8,128]{1,0:T(8,128)S(1)} %collective-permute-done.1.refs_1_, s32[8,128]{1,0:T(8,128)S(1)} %collective-permute-done.2.refs_2_, s32[8,128]{1,0:T(8,128)S(1)} %collective-permute-done.3.refs_3_, ...), custom_call_target="tpu_custom_call" | custom-call | flops 1342177280 | bytes 1048576 | tf_op jit(solution)/shard_map/place/pallas_call | solution.py:341
  108.3 3.4 %place.3 = (f32[1024,256]{1,0:T(8,128)S(1)}, f32[1024,256]{1,0:T(8,128)}) custom-call(s32[3]{0:T(128)S(1)} %pad_add_fusion.3.where_ref, s32[8,128]{1,0:T(8,128)S(1)} %get-tuple-element.34.refs_0_, s32[8,128]{1,0:T(8,128)S(1)} %collective-permute-done.1.refs_1_, s32[8,128]{1,0:T(8,128)S(1)} %collective-permute-done.2.refs_2_, ...), custom_call_target="tpu_custom_call" | custom-call | flops 1342177280 | bytes 1048576 | tf_op jit(solution)/shard_map/place/pallas_call | solution.py:341
  111.7 2.0 %collective-permute-done.32 = bf16[528,256]{1,0:T(8,128)(2,1)S(1)} collective-permute-done((bf16[528,256]{1,0:T(8,128)(2,1)S(1)}, bf16[528,256]{1,0:T(8,128)(2,1)S(1)}, u32[]{:S(2)}, u32[]{:S(2)}) %collective-permute-start.32) | collective-permute-done | bytes 270368 | tf_op jit(solution)/shard_map/ppermute | solution.py:441
  113.7 1.3 %add_bitcast_fusion = f32[1,1024,256]{2,1,0:T(8,128)} fusion(f32[1024,256]{1,0:T(8,128)S(1)} %get-tuple-element.61, f32[1024,256]{1,0:T(8,128)S(1)} %get-tuple-element.49, bf16[1024,256]{1,0:T(8,128)(2,1)S(1)} %collective-permute-done.22, bf16[544,256]{1,0:T(8,128)(2,1)S(1)} %collective-permute-done.26, bf16[480,256]{1,0:T(8,128)(2,1)S(1)} %collective-permute-done.24, ...), kind=kLoop, calls=%fused_computation.2 | loop fusion | flops 3407872 | bytes 4718592 | tf_op jit(solution)/shard_map/broadcast_in_dim | solution.py:462
  (80 shorter events, 3.7 us)
Async XLA Ops:
  6.8 0.9 copy-start.2
  7.1 17.8 %copy-start = (bf16[1,4096,256]{2,1,0:T(8,128)(2,1)S(1)}, bf16[1,4096,256]{2,1,0:T(8,128)(2,1)}, u32[]{:S(2)}) copy-start(bf16[1,4096,256]{2,1,0:T(8,128)(2,1)} %param.5) | copy-start | bytes 6291460
  7.1 17.8 %copy-start.1 = (f32[3,3]{1,0:T(4,128)S(1)}, f32[3,3]{1,0:T(4,128)}, u32[]{:S(2)}) copy-start(f32[3,3]{1,0:T(4,128)} %k_ref.5) | copy-start | bytes 112
  7.1 1.7 %collective-permute-start = (bf16[4,128,256]{2,1,0:T(8,128)(2,1)S(1)}, bf16[4,128,256]{2,1,0:T(8,128)(2,1)S(1)}, u32[]{:S(2)}, u32[]{:S(2)}) collective-permute-start(bf16[4,128,256]{2,1,0:T(8,128)(2,1)S(1)} %bitcast.109), channel_id=1, source_target_pairs={{0,4},{4,0},{8,12},{12,8},{16,20},{20,16},{24,28},{28,24},{1,5},{5... | collective-permute-start | bytes 786440 | tf_op jit(solution)/shard_map/ppermute | solution.py:367
  8.9 5.3 %collective-permute-start.4 = (bf16[128,256]{1,0:T(8,128)(2,1)S(1)}, bf16[128,256]{1,0:T(8,128)(2,1)S(1)}, u32[]{:S(2)}, u32[]{:S(2)}) collective-permute-start(bf16[128,256]{1,0:T(8,128)(2,1)S(1)} %get-tuple-element.72), channel_id=1, source_target_pairs={{0,8},{4,12},{8,0},{12,4},{16,24},{20,28},{24,16},{28,20},{1,9},{5... | collective-permute-start | bytes 196616 | tf_op jit(solution)/shard_map/ppermute | solution.py:367
  11.9 4.3 %collective-permute-start.5 = (bf16[128,256]{1,0:T(8,128)(2,1)S(1)}, bf16[128,256]{1,0:T(8,128)(2,1)S(1)}, u32[]{:S(2)}, u32[]{:S(2)}) collective-permute-start(bf16[128,256]{1,0:T(8,128)(2,1)S(1)} %get-tuple-element.74), channel_id=1, source_target_pairs={{0,16},{4,20},{8,24},{12,28},{16,0},{20,4},{24,8},{28,12},{1,17},{... | collective-permute-start | bytes 196616 | tf_op jit(solution)/shard_map/ppermute | solution.py:367
  13.4 5.2 %collective-permute-start.6 = (bf16[128,256]{1,0:T(8,128)(2,1)S(1)}, bf16[128,256]{1,0:T(8,128)(2,1)S(1)}, u32[]{:S(2)}, u32[]{:S(2)}) collective-permute-start(bf16[128,256]{1,0:T(8,128)(2,1)S(1)} %get-tuple-element.73), channel_id=1, source_target_pairs={{0,24},{4,28},{8,16},{12,20},{16,8},{20,12},{24,0},{28,4},{1,25},{... | collective-permute-start | bytes 196616 | tf_op jit(solution)/shard_map/ppermute | solution.py:367
  18.6 4.3 %collective-permute-start.7 = (bf16[128,256]{1,0:T(8,128)(2,1)S(1)}, bf16[128,256]{1,0:T(8,128)(2,1)S(1)}, u32[]{:S(2)}, u32[]{:S(2)}) collective-permute-start(bf16[128,256]{1,0:T(8,128)(2,1)S(1)} %fusion.5), channel_id=1, source_target_pairs={{0,8},{4,12},{8,0},{12,4},{16,24},{20,28},{24,16},{28,20},{1,9},{5... | collective-permute-start | bytes 196616 | tf_op jit(solution)/shard_map/ppermute | solution.py:367
  19.2 4.3 %collective-permute-start.8 = (bf16[128,256]{1,0:T(8,128)(2,1)S(1)}, bf16[128,256]{1,0:T(8,128)(2,1)S(1)}, u32[]{:S(2)}, u32[]{:S(2)}) collective-permute-start(bf16[128,256]{1,0:T(8,128)(2,1)S(1)} %fusion.5), channel_id=1, source_target_pairs={{0,16},{4,20},{8,24},{12,28},{16,0},{20,4},{24,8},{28,12},{1,17},{... | collective-permute-start | bytes 196616 | tf_op jit(solution)/shard_map/ppermute | solution.py:367
  19.6 5.2 %collective-permute-start.9 = (bf16[128,256]{1,0:T(8,128)(2,1)S(1)}, bf16[128,256]{1,0:T(8,128)(2,1)S(1)}, u32[]{:S(2)}, u32[]{:S(2)}) collective-permute-start(bf16[128,256]{1,0:T(8,128)(2,1)S(1)} %fusion.5), channel_id=1, source_target_pairs={{0,24},{4,28},{8,16},{12,20},{16,8},{20,12},{24,0},{28,4},{1,25},{... | collective-permute-start | bytes 196616 | tf_op jit(solution)/shard_map/ppermute | solution.py:367
  24.8 5.4 %collective-permute-start.10 = (bf16[4,128,256]{2,1,0:T(8,128)(2,1)S(1)}, bf16[4,128,256]{2,1,0:T(8,128)(2,1)S(1)}, u32[]{:S(2)}, u32[]{:S(2)}) collective-permute-start(bf16[4,128,256]{2,1,0:T(8,128)(2,1)S(1)} %pad_maximum_fusion.1), channel_id=1, source_target_pairs={{0,4},{4,0},{8,12},{12,8},{16,20},{20,16},{24,28},{28,24},{1,5},{5... | collective-permute-start | bytes 786440 | tf_op jit(solution)/shard_map/ppermute | solution.py:367
  35.1 5.4 %collective-permute-start.11 = (f32[512,256]{1,0:T(8,128)S(1)}, f32[512,256]{1,0:T(8,128)S(1)}, u32[]{:S(2)}, u32[]{:S(2)}) collective-permute-start(f32[512,256]{1,0:T(8,128)S(1)} %get-tuple-element.45), channel_id=1, source_target_pairs={{0,4},{4,0},{8,12},{12,8},{16,20},{20,16},{24,28},{28,24},{1,5},{5... | collective-permute-start | bytes 1572872 | tf_op jit(solution)/shard_map/ppermute | solution.py:367
  40.6 5.8 %collective-permute-start.12 = (f32[128,256]{1,0:T(8,128)S(1)}, f32[128,256]{1,0:T(8,128)S(1)}, u32[]{:S(2)}, u32[]{:S(2)}) collective-permute-start(f32[128,256]{1,0:T(8,128)S(1)} %get-tuple-element.67), channel_id=1, source_target_pairs={{0,8},{4,12},{8,0},{12,4},{16,24},{20,28},{24,16},{28,20},{1,9},{5... | collective-permute-start | bytes 393224 | tf_op jit(solution)/shard_map/ppermute | solution.py:367
  42.3 8.0 %collective-permute-start.13 = (f32[128,256]{1,0:T(8,128)S(1)}, f32[128,256]{1,0:T(8,128)S(1)}, u32[]{:S(2)}, u32[]{:S(2)}) collective-permute-start(f32[128,256]{1,0:T(8,128)S(1)} %get-tuple-element.69), channel_id=1, source_target_pairs={{0,16},{4,20},{8,24},{12,28},{16,0},{20,4},{24,8},{28,12},{1,17},{... | collective-permute-start | bytes 393224 | tf_op jit(solution)/shard_map/ppermute | solution.py:367
  43.8 6.4 %collective-permute-start.14 = (f32[128,256]{1,0:T(8,128)S(1)}, f32[128,256]{1,0:T(8,128)S(1)}, u32[]{:S(2)}, u32[]{:S(2)}) collective-permute-start(f32[128,256]{1,0:T(8,128)S(1)} %get-tuple-element.68), channel_id=1, source_target_pairs={{0,24},{4,28},{8,16},{12,20},{16,8},{20,12},{24,0},{28,4},{1,25},{... | collective-permute-start | bytes 393224 | tf_op jit(solution)/shard_map/ppermute | solution.py:367
  50.3 4.9 %collective-permute-start.15 = (bf16[128,256]{1,0:T(8,128)(2,1)S(1)}, bf16[128,256]{1,0:T(8,128)(2,1)S(1)}, u32[]{:S(2)}, u32[]{:S(2)}) collective-permute-start(bf16[128,256]{1,0:T(8,128)(2,1)S(1)} %get-tuple-element.63), channel_id=1, source_target_pairs={{0,1},{1,0},{2,3},{3,2},{4,5},{5,4},{6,7},{7,6},{8,9},{9,8},{10,11... | collective-permute-start | bytes 196616 | tf_op jit(solution)/shard_map/ppermute | solution.py:370
  51.9 6.6 %collective-permute-start.16 = (bf16[128,256]{1,0:T(8,128)(2,1)S(1)}, bf16[128,256]{1,0:T(8,128)(2,1)S(1)}, u32[]{:S(2)}, u32[]{:S(2)}) collective-permute-start(bf16[128,256]{1,0:T(8,128)(2,1)S(1)} %get-tuple-element.63), channel_id=1, source_target_pairs={{0,2},{1,3},{2,0},{3,1},{4,6},{5,7},{6,4},{7,5},{8,10},{9,11},{10,... | collective-permute-start | bytes 196616 | tf_op jit(solution)/shard_map/ppermute | solution.py:370
  54.5 6.1 %collective-permute-start.17 = (bf16[128,256]{1,0:T(8,128)(2,1)S(1)}, bf16[128,256]{1,0:T(8,128)(2,1)S(1)}, u32[]{:S(2)}, u32[]{:S(2)}) collective-permute-start(bf16[128,256]{1,0:T(8,128)(2,1)S(1)} %get-tuple-element.63), channel_id=1, source_target_pairs={{0,3},{1,2},{2,1},{3,0},{4,7},{5,6},{6,5},{7,4},{8,11},{9,10},{10,... | collective-permute-start | bytes 196616 | tf_op jit(solution)/shard_map/ppermute | solution.py:370
  60.6 16.1 %collective-permute-start.18 = (bf16[5,128,256]{2,1,0:T(8,128)(2,1)S(1)}, bf16[5,128,256]{2,1,0:T(8,128)(2,1)S(1)}, u32[]{:S(2)}, u32[]{:S(2)}) collective-permute-start(bf16[5,128,256]{2,1,0:T(8,128)(2,1)S(1)} %bitcast_dynamic-update-slice_fusion), channel_id=1, source_target_pairs={{0,8},{4,12},{8,0},{12,4},{16,24},{20,28},{24,16},{28,20},{1,9},{5... | collective-permute-start | bytes 983048 | tf_op jit(solution)/shard_map/ppermute | solution.py:367
  61.8 15.0 %collective-permute-start.19 = (bf16[5,128,256]{2,1,0:T(8,128)(2,1)S(1)}, bf16[5,128,256]{2,1,0:T(8,128)(2,1)S(1)}, u32[]{:S(2)}, u32[]{:S(2)}) collective-permute-start(bf16[5,128,256]{2,1,0:T(8,128)(2,1)S(1)} %bitcast_dynamic-update-slice_fusion), channel_id=1, source_target_pairs={{0,16},{4,20},{8,24},{12,28},{16,0},{20,4},{24,8},{28,12},{1,17},{... | collective-permute-start | bytes 983048 | tf_op jit(solution)/shard_map/ppermute | solution.py:367
  62.6 17.6 %collective-permute-start.20 = (bf16[5,128,256]{2,1,0:T(8,128)(2,1)S(1)}, bf16[5,128,256]{2,1,0:T(8,128)(2,1)S(1)}, u32[]{:S(2)}, u32[]{:S(2)}) collective-permute-start(bf16[5,128,256]{2,1,0:T(8,128)(2,1)S(1)} %bitcast_dynamic-update-slice_fusion), channel_id=1, source_target_pairs={{0,24},{4,28},{8,16},{12,20},{16,8},{20,12},{24,0},{28,4},{1,25},{... | collective-permute-start | bytes 983048 | tf_op jit(solution)/shard_map/ppermute | solution.py:367
  64.1 27.5 %collective-permute-start.1 = (s32[8,128]{1,0:T(8,128)S(1)}, s32[8,128]{1,0:T(8,128)S(1)}, u32[]{:S(2)}, u32[]{:S(2)}) collective-permute-start(s32[8,128]{1,0:T(8,128)S(1)} %get-tuple-element.34.refs_0_), channel_id=1, source_target_pairs={{0,1},{1,0},{2,3},{3,2},{4,5},{5,4},{6,7},{7,6},{8,9},{9,8},{10,11... | collective-permute-start | bytes 12296 | tf_op jit(solution)/shard_map/ppermute | solution.py:370
  66.0 15.7 %collective-permute-start.27 = (bf16[496,256]{1,0:T(8,128)(2,1)S(1)}, bf16[496,256]{1,0:T(8,128)(2,1)S(1)}, u32[]{:S(2)}, u32[]{:S(2)}) collective-permute-start(bf16[496,256]{1,0:T(8,128)(2,1)S(1)} %get-tuple-element.57), channel_id=1, source_target_pairs={{3,2},{0,1},{7,6},{4,5},{11,10},{8,9},{15,14},{12,13},{19,18},{16,... | collective-permute-start | bytes 761864 | tf_op jit(solution)/shard_map/ppermute | solution.py:441
  76.7 25.2 %collective-permute-start.2 = (s32[8,128]{1,0:T(8,128)S(1)}, s32[8,128]{1,0:T(8,128)S(1)}, u32[]{:S(2)}, u32[]{:S(2)}) collective-permute-start(s32[8,128]{1,0:T(8,128)S(1)} %get-tuple-element.34.refs_0_), channel_id=1, source_target_pairs={{0,2},{1,3},{2,0},{3,1},{4,6},{5,7},{6,4},{7,5},{8,10},{9,11},{10,... | collective-permute-start | bytes 12296 | tf_op jit(solution)/shard_map/ppermute | solution.py:370
  76.8 8.4 %collective-permute-start.30 = (bf16[528,256]{1,0:T(8,128)(2,1)S(1)}, bf16[528,256]{1,0:T(8,128)(2,1)S(1)}, u32[]{:S(2)}, u32[]{:S(2)}) collective-permute-start(bf16[528,256]{1,0:T(8,128)(2,1)S(1)} %get-tuple-element.60), channel_id=1, source_target_pairs={{3,2},{0,1},{7,6},{4,5},{11,10},{8,9},{15,14},{12,13},{19,18},{16,... | collective-permute-start | bytes 811016 | tf_op jit(solution)/shard_map/ppermute | solution.py:441
  80.3 7.9 %collective-permute-start.25 = (bf16[544,256]{1,0:T(8,128)(2,1)S(1)}, bf16[544,256]{1,0:T(8,128)(2,1)S(1)}, u32[]{:S(2)}, u32[]{:S(2)}) collective-permute-start(bf16[544,256]{1,0:T(8,128)(2,1)S(1)} %get-tuple-element.54), channel_id=1, source_target_pairs={{3,2},{0,1},{7,6},{4,5},{11,10},{8,9},{15,14},{12,13},{19,18},{16,... | collective-permute-start | bytes 835592 | tf_op jit(solution)/shard_map/ppermute | solution.py:441
  81.8 23.6 %collective-permute-start.21 = (bf16[4,5,128,256]{3,2,1,0:T(8,128)(2,1)S(1)}, bf16[4,5,128,256]{3,2,1,0:T(8,128)(2,1)S(1)}, u32[]{:S(2)}, u32[]{:S(2)}) collective-permute-start(bf16[4,5,128,256]{3,2,1,0:T(8,128)(2,1)S(1)} %pad_maximum_fusion.refs_4_.refs_5_), channel_id=1, source_target_pairs={{0,4},{4,0},{8,12},{12,8},{16,20},{20,16},{24,28},{28,24},{1,5},{5... | collective-permute-start | bytes 3932168 | tf_op jit(solution)/shard_map/ppermute | solution.py:367
  85.1 3.8 %collective-permute-start.28 = (bf16[496,256]{1,0:T(8,128)(2,1)S(1)}, bf16[496,256]{1,0:T(8,128)(2,1)S(1)}, u32[]{:S(2)}, u32[]{:S(2)}) collective-permute-start(bf16[496,256]{1,0:T(8,128)(2,1)S(1)} %add_convert_fusion.4), channel_id=1, source_target_pairs={{2,1},{1,2},{6,5},{5,6},{10,9},{9,10},{14,13},{13,14},{18,17},{17,... | collective-permute-start | bytes 761864 | tf_op jit(solution)/shard_map/ppermute | solution.py:441
  88.2 11.3 %collective-permute-start.31 = (bf16[528,256]{1,0:T(8,128)(2,1)S(1)}, bf16[528,256]{1,0:T(8,128)(2,1)S(1)}, u32[]{:S(2)}, u32[]{:S(2)}) collective-permute-start(bf16[528,256]{1,0:T(8,128)(2,1)S(1)} %add_convert_fusion.2), channel_id=1, source_target_pairs={{2,1},{1,2},{6,5},{5,6},{10,9},{9,10},{14,13},{13,14},{18,17},{17,... | collective-permute-start | bytes 811016 | tf_op jit(solution)/shard_map/ppermute | solution.py:441
  88.9 13.7 %collective-permute-start.3 = (s32[8,128]{1,0:T(8,128)S(1)}, s32[8,128]{1,0:T(8,128)S(1)}, u32[]{:S(2)}, u32[]{:S(2)}) collective-permute-start(s32[8,128]{1,0:T(8,128)S(1)} %get-tuple-element.34.refs_0_), channel_id=1, source_target_pairs={{0,3},{1,2},{2,1},{3,0},{4,7},{5,6},{6,5},{7,4},{8,11},{9,10},{10,... | collective-permute-start | bytes 12296 | tf_op jit(solution)/shard_map/ppermute | solution.py:370
  91.6 12.3 %collective-permute-start.23 = (bf16[480,256]{1,0:T(8,128)(2,1)S(1)}, bf16[480,256]{1,0:T(8,128)(2,1)S(1)}, u32[]{:S(2)}, u32[]{:S(2)}) collective-permute-start(bf16[480,256]{1,0:T(8,128)(2,1)S(1)} %get-tuple-element.52), channel_id=1, source_target_pairs={{3,2},{0,1},{7,6},{4,5},{11,10},{8,9},{15,14},{12,13},{19,18},{16,... | collective-permute-start | bytes 737288 | tf_op jit(solution)/shard_map/ppermute | solution.py:441
  99.5 12.2 %collective-permute-start.22 = (bf16[1024,256]{1,0:T(8,128)(2,1)S(1)}, bf16[1024,256]{1,0:T(8,128)(2,1)S(1)}, u32[]{:S(2)}, u32[]{:S(2)}) collective-permute-start(bf16[1024,256]{1,0:T(8,128)(2,1)S(1)} %get-tuple-element.50), channel_id=1, source_target_pairs={{3,2},{0,1},{7,6},{4,5},{11,10},{8,9},{15,14},{12,13},{19,18},{16,... | collective-permute-start | bytes 1572872 | tf_op jit(solution)/shard_map/ppermute | solution.py:441
  101.9 9.8 %collective-permute-start.26 = (bf16[544,256]{1,0:T(8,128)(2,1)S(1)}, bf16[544,256]{1,0:T(8,128)(2,1)S(1)}, u32[]{:S(2)}, u32[]{:S(2)}) collective-permute-start(bf16[544,256]{1,0:T(8,128)(2,1)S(1)} %add_convert_fusion), channel_id=1, source_target_pairs={{2,1},{1,2},{6,5},{5,6},{10,9},{9,10},{14,13},{13,14},{18,17},{17,... | collective-permute-start | bytes 835592 | tf_op jit(solution)/shard_map/ppermute | solution.py:441
  102.6 9.1 %collective-permute-start.29 = (bf16[496,256]{1,0:T(8,128)(2,1)S(1)}, bf16[496,256]{1,0:T(8,128)(2,1)S(1)}, u32[]{:S(2)}, u32[]{:S(2)}) collective-permute-start(bf16[496,256]{1,0:T(8,128)(2,1)S(1)} %add_convert_fusion.3), channel_id=1, source_target_pairs={{1,0},{2,3},{5,4},{6,7},{9,8},{10,11},{13,12},{14,15},{17,16},{18,... | collective-permute-start | bytes 761864 | tf_op jit(solution)/shard_map/ppermute | solution.py:441
  104.0 9.8 %collective-permute-start.32 = (bf16[528,256]{1,0:T(8,128)(2,1)S(1)}, bf16[528,256]{1,0:T(8,128)(2,1)S(1)}, u32[]{:S(2)}, u32[]{:S(2)}) collective-permute-start(bf16[528,256]{1,0:T(8,128)(2,1)S(1)} %add_convert_fusion.1), channel_id=1, source_target_pairs={{1,0},{2,3},{5,4},{6,7},{9,8},{10,11},{13,12},{14,15},{17,16},{18,... | collective-permute-start | bytes 811016 | tf_op jit(solution)/shard_map/ppermute | solution.py:441
  105.3 6.4 %collective-permute-start.24 = (bf16[480,256]{1,0:T(8,128)(2,1)S(1)}, bf16[480,256]{1,0:T(8,128)(2,1)S(1)}, u32[]{:S(2)}, u32[]{:S(2)}) collective-permute-start(bf16[480,256]{1,0:T(8,128)(2,1)S(1)} %add_convert_fusion.5), channel_id=1, source_target_pairs={{2,1},{1,2},{6,5},{5,6},{10,9},{9,10},{14,13},{13,14},{18,17},{17,... | collective-permute-start | bytes 737288 | tf_op jit(solution)/shard_map/ppermute | solution.py:441
